TPU v7x, 32 devices: a whole 2x2x4 slice. The times are simulated.
32 devices in a mesh: dp: 4 (over y, x), ctx: 8 (over z, core).
Axes of the slice: x: 2, y: 2, z: 4, core: 2. Of those that a mesh axis runs over, the one named last changes fastest.
Arguments:
- tokens: bfloat16 [4, 1024, 2048], P('dp', 'ctx'), may hold values from -6 to 6
- positions: int32 [4, 1024], P('dp', 'ctx'), may hold values from 0 to 1023, as said below
- norm_gain: float32 [2048], replicated, may hold values from 0.5 to 1.5
- norm_bias: float32 [2048], replicated, may hold values from -1.8 to 1.8
- qkv_weight: bfloat16 [2048, 6144], P('ctx'), may hold values from -0.125 to 0.125
- qkv_bias: float32 [6144], replicated, may hold values from -1.8 to 1.8
- dense_weight: bfloat16 [2048, 2048], P('ctx'), may hold values from -2 to 2
- dense_bias: float32 [2048], replicated, may hold values from -1.8 to 1.8
- up_weight: bfloat16 [2048, 8192], P('ctx'), may hold values from -0.125 to 0.125
- up_bias: float32 [8192], replicated, may hold values from -1.8 to 1.8
- down_weight: bfloat16 [8192, 2048], P('ctx'), may hold values from -0.0625 to 0.0625
- down_bias: float32 [2048], replicated, may hold values from -1.8 to 1.8
- clip_limit: int32 [32], replicated, may hold values from 3 to 11
- cotangent: bfloat16 [4, 1024, 2048], P('dp', 'ctx'), may hold values from -6 to 6
Outputs:
- layer_out: bfloat16 [4, 1024, 2048], P('dp', 'ctx')
- tokens_grad: float32 [4, 1024, 2048], P('dp', 'ctx')
- norm_gain_grad: float32 [2048], replicated
- norm_bias_grad: float32 [2048], replicated
- qkv_weight_grad: float32 [2048, 6144], P('ctx')
- qkv_bias_grad: float32 [6144], replicated
- dense_weight_grad: float32 [2048, 2048], P('ctx')
- dense_bias_grad: float32 [2048], replicated
- up_weight_grad: float32 [2048, 8192], P('ctx')
- up_bias_grad: float32 [8192], replicated
- down_weight_grad: float32 [8192, 2048], P('ctx')
- down_bias_grad: float32 [2048], replicated
- head_maxima: float32 [32], replicated
- clipped_weight: float32 [2048, 4096], P('ctx')
- clipped_bias: float32 [4096], replicated
Inputs may be any that keep to these rules, and one draw needn't show every extreme that they name: `positions`: within each sequence the ids rise by one from 0 at its first token and return to 0 at the first token of each packed document; the first sequence holds a single document.
All inputs are finite; a program needn't handle non-finite values.
Results may differ from a plain program's by a relative error of at most 0.017.
Values may be sent and summed in bfloat16 or wider, within the bound.
No kernel may reach another device: no remote copies, remote signals or barrier semaphores. Data moves between devices by JAX's collectives and lax.ppermute only.
A program may use at most 512 MiB of HBM per device.

v0:
```python
from functools import partial
import jax
import jax.numpy as jnp
from jax import lax
from jax.sharding import PartitionSpec as P

ROT = 32
EPSILON = 1e-05
MASKED = -1e30
ROPE_BASE = 10000.0
BF16 = jnp.bfloat16
F32 = jnp.float32


def rotary_tables(positions):
    half_rot = ROT // 2
    frequency = ROPE_BASE ** (-(jnp.arange(half_rot, dtype=F32) * 2.0 / ROT))
    angles = positions.astype(F32)[..., None] * frequency
    cosine = jnp.cos(angles)
    sine = jnp.sin(angles)
    return (
        jnp.concatenate([cosine, cosine], -1)[..., None, :],
        jnp.concatenate([sine, sine], -1)[..., None, :],
    )


def rotate(values, cosine, sine):
    half_rot = ROT // 2
    turned = values[..., :ROT]
    swapped = jnp.concatenate([-turned[..., half_rot:], turned[..., :half_rot]], -1)
    return jnp.concatenate([turned * cosine + swapped * sine, values[..., ROT:]], -1)


def rotate_back(gradient, cosine, sine):
    half_rot = ROT // 2
    turned = gradient[..., :ROT]
    scaled = turned * sine
    swapped = jnp.concatenate([scaled[..., half_rot:], -scaled[..., :half_rot]], -1)
    return jnp.concatenate([turned * cosine + swapped, gradient[..., ROT:]], -1)


def dot(left, right, contract):
    return lax.dot_general(
        left, right, ((contract[:1], contract[1:]), ((), ())), preferred_element_type=F32
    )


def per_device(
    tokens,
    positions,
    norm_gain,
    norm_bias,
    qkv_weight,
    qkv_bias,
    dense_weight,
    dense_bias,
    up_weight,
    up_bias,
    down_weight,
    down_bias,
    clip_limit,
    cotangent,
):
    seqs, stretch, width = tokens.shape
    heads = clip_limit.shape[0]
    head_dim = width // heads
    rows = seqs * stretch
    parts = lax.axis_size("ctx")
    part = lax.axis_index("ctx")
    own_heads = heads // parts
    own = own_heads * head_dim
    own_rows = qkv_weight.shape[0]
    own_ff = down_weight.shape[0]
    length = stretch * parts
    all_rows = seqs * length
    scale = head_dim ** (-0.5)
    pieces = jnp.concatenate(
        [
            qkv_weight.reshape(own_rows, 3, parts, own)
            .transpose(2, 0, 1, 3)
            .reshape(parts, own_rows, 3 * own),
            up_weight.reshape(own_rows, parts, own_ff).transpose(1, 0, 2),
        ],
        axis=2,
    )
    in_weight = lax.all_to_all(pieces, "ctx", split_axis=0, concat_axis=0, tiled=True).reshape(
        width, 3 * own + own_ff
    )
    grad_rows = lax.all_gather(cotangent, "ctx", axis=1, tiled=True).reshape(all_rows, width)
    inputs = tokens.reshape(rows, width).astype(F32)
    centre = inputs - jnp.mean(inputs, axis=-1, keepdims=True)
    inv_std = lax.rsqrt(jnp.mean(centre * centre, axis=-1, keepdims=True) + EPSILON)
    normed = centre * inv_std
    hidden_local = (normed * norm_gain + norm_bias).astype(BF16)
    hidden = lax.all_gather(
        hidden_local.reshape(seqs, stretch, width), "ctx", axis=1, tiled=True
    ).reshape(all_rows, width)
    all_positions = lax.all_gather(positions, "ctx", axis=1, tiled=True)
    qkv_own_bias = lax.dynamic_slice_in_dim(
        qkv_bias.reshape(3, parts, own), part, 1, axis=1
    ).reshape(3 * own)
    up_own_bias = lax.dynamic_slice_in_dim(up_bias, part * own_ff, own_ff)
    projected = dot(hidden, in_weight, (1, 0))
    joined = projected[:, : 3 * own] + qkv_own_bias
    upward = projected[:, 3 * own :] + up_own_bias
    cosine, sine = rotary_tables(all_positions)
    shaped = joined.reshape(seqs, length, 3, own_heads, head_dim)
    queries = rotate(shaped[:, :, 0], cosine, sine).astype(BF16)
    keys = rotate(shaped[:, :, 1], cosine, sine).astype(BF16)
    values = shaped[:, :, 2].astype(BF16)
    place = jnp.arange(length, dtype=jnp.int32)
    allowed = place[:, None] >= place[None, :]
    scores = jnp.einsum("sqhd,skhd->shqk", queries, keys, preferred_element_type=F32) * scale
    scores = jnp.where(allowed, scores, MASKED)
    row_max = jnp.max(scores, axis=-1, keepdims=True)
    expo = jnp.exp(scores - row_max)
    row_sum = jnp.sum(expo, axis=-1, keepdims=True)
    probs = expo / row_sum
    probs_low = probs.astype(BF16)
    mixed = jnp.einsum("shqk,skhd->sqhd", probs_low, values, preferred_element_type=F32)
    attended = mixed.reshape(all_rows, own).astype(BF16)
    own_maxima = jnp.max(row_max, axis=(0, 2, 3))
    slots = lax.dynamic_update_slice_in_dim(
        jnp.full((heads,), MASKED, F32), own_maxima, part * own_heads, axis=0
    )
    head_maxima = lax.pmax(slots, ("dp", "ctx"))
    activated = jax.nn.gelu(upward, approximate=True).astype(BF16)
    branch = dot(attended, dense_weight, (1, 0)) + dot(activated, down_weight, (1, 0))
    branch_sum = lax.psum_scatter(
        branch.astype(BF16).reshape(seqs, length, width), "ctx", scatter_dimension=1, tiled=True
    ).reshape(rows, width)
    layer_out = (inputs + branch_sum.astype(F32) + dense_bias + down_bias).astype(BF16)
    mixed_grad = dot(grad_rows, dense_weight, (1, 1)).astype(BF16)
    act_grad = dot(grad_rows, down_weight, (1, 1))
    dense_grad = dot(attended, grad_rows, (0, 0))
    down_grad = dot(activated, grad_rows, (0, 0))
    out_bias_grad = jnp.sum(cotangent.reshape(rows, width).astype(F32), axis=0)
    unused_value, gelu_back = jax.vjp(partial(jax.nn.gelu, approximate=True), upward)
    up_low = gelu_back(act_grad)[0].astype(BF16)
    mixed_low = mixed_grad.reshape(seqs, length, own_heads, head_dim)
    value_grad = jnp.einsum("shqk,sqhd->skhd", probs_low, mixed_low, preferred_element_type=F32)
    prob_grad = jnp.einsum("sqhd,skhd->shqk", mixed_low, values, preferred_element_type=F32)
    delta = jnp.sum(probs * prob_grad, axis=-1, keepdims=True)
    score_grad = (probs * (prob_grad - delta)).astype(BF16)
    query_grad = jnp.einsum("shqk,skhd->sqhd", score_grad, keys, preferred_element_type=F32) * scale
    key_grad = (
        jnp.einsum("shqk,sqhd->skhd", score_grad, queries, preferred_element_type=F32) * scale
    )
    joined_low = (
        jnp.stack(
            [
                rotate_back(query_grad, cosine, sine),
                rotate_back(key_grad, cosine, sine),
                value_grad,
            ],
            axis=2,
        )
        .reshape(all_rows, 3 * own)
        .astype(BF16)
    )
    both = jnp.concatenate([joined_low, up_low], axis=1)
    hidden_part = dot(both, in_weight, (1, 1))
    hidden_grad = (
        lax.psum_scatter(
            hidden_part.astype(BF16).reshape(seqs, length, width),
            "ctx",
            scatter_dimension=1,
            tiled=True,
        )
        .reshape(rows, width)
        .astype(F32)
    )
    in_grad = dot(hidden, both, (0, 0)).astype(BF16)
    in_quarter = lax.psum_scatter(
        in_grad.reshape(parts, own_rows, 3 * own + own_ff), "dp", scatter_dimension=1, tiled=True
    )
    in_quarter = lax.all_to_all(in_quarter, "ctx", split_axis=0, concat_axis=0, tiled=True)
    in_rows = lax.all_gather(in_quarter.transpose(1, 0, 2), "dp", axis=0, tiled=True)
    qkv_grad = (
        in_rows[:, :, : 3 * own]
        .reshape(own_rows, parts, 3, own)
        .transpose(0, 2, 1, 3)
        .reshape(own_rows, 3 * width)
        .astype(F32)
    )
    up_grad = in_rows[:, :, 3 * own :].reshape(own_rows, parts * own_ff).astype(F32)
    out_grad = lax.psum(jnp.concatenate([dense_grad, down_grad], axis=0).astype(BF16), "dp")
    gain_part = jnp.sum(hidden_grad * normed, axis=0)
    shift_part = jnp.sum(hidden_grad, axis=0)
    scaled = hidden_grad * norm_gain
    tokens_grad = cotangent.reshape(rows, width).astype(F32) + inv_std * (
        scaled
        - jnp.mean(scaled, axis=-1, keepdims=True)
        - normed * jnp.mean(scaled * normed, axis=-1, keepdims=True)
    )
    qkv_bias_part = lax.dynamic_update_slice(
        jnp.zeros((3, parts, own), F32),
        jnp.sum(joined_low.astype(F32), axis=0).reshape(3, 1, own),
        (0, part, 0),
    ).reshape(3 * width)
    up_bias_part = lax.dynamic_update_slice(
        jnp.zeros((parts * own_ff,), F32), jnp.sum(up_low.astype(F32), axis=0), (part * own_ff,)
    )
    gain_grad, shift_grad, qkv_bias_grad, out_bias_grad, up_bias_grad = lax.psum(
        (gain_part, shift_part, qkv_bias_part, out_bias_grad, up_bias_part), ("dp", "ctx")
    )
    limits = clip_limit.astype(F32)
    factor = limits / jnp.maximum(head_maxima, limits)
    column_scale = jnp.tile(jnp.repeat(jnp.sqrt(factor), head_dim), 2)
    clipped_weight = qkv_weight[:, : 2 * width].astype(F32) * column_scale
    clipped_bias = qkv_bias[: 2 * width] * column_scale
    return (
        layer_out.reshape(seqs, stretch, width),
        tokens_grad.reshape(seqs, stretch, width),
        gain_grad,
        shift_grad,
        qkv_grad,
        qkv_bias_grad,
        out_grad[:own].astype(F32),
        out_bias_grad,
        up_grad,
        up_bias_grad,
        out_grad[own:].astype(F32),
        out_bias_grad,
        head_maxima,
        clipped_weight,
        clipped_bias,
    )


def solution(mesh):
    rows = P("dp", "ctx", None)
    weight = P("ctx", None)
    in_specs = (rows, P("dp", "ctx"), P(), P()) + (weight, P()) * 4 + (P(), rows)
    out_specs = (rows, rows, P(), P()) + (weight, P()) * 4 + (P(), weight, P())
    return jax.shard_map(
        per_device, mesh=mesh, in_specs=in_specs, out_specs=out_specs, check_vma=False
    )
```

profile of v0, /device:TPU:0, one launch (start us, length us, event | category | flops | bytes accessed | tf_op | source)
XLA Modules:
  0.0 971.7 jit_solution(4422547686251745322)
XLA Ops:
  7.9 4.6 copy.74
  12.6 3.9 copy.75
  16.4 6.4 copy.76
  22.9 6.7 pad_maximum_fusion
  29.6 6.5 all-to-all-start
  38.6 174.2 %all_gather.13 = s32[1,1024]{1,0:T(1,128)S(1)} all-gather(s32[1,128]{1,0:T(1,128)S(1)} %copy-done.37), channel_id=1, replica_groups=mesh['dp'=4,'ctx'=8] {'ctx'}, dimensions={1}, use_global_device_ids=true | all-gather | bytes 4608 | tf_op jit(solution)/shard_map/all_gather | solution.py:98
  214.9 4.6 fusion.47
  219.5 29.4 %all-to-all-done = bf16[8,256,1792]{1,2,0:T(8,128)(2,1)} async-done(((bf16[8,256,1792]{1,2,0:T(8,128)(2,1)}), bf16[8,256,1792]{1,2,0:T(8,128)(2,1)}, u32[]{:S(2)}, u32[]{:S(2)}) %all-to-all-start) | async-done | bytes 7340064 | tf_op jit(solution)/shard_map/all_to_all | solution.py:86
  248.9 9.9 %copy.77 = bf16[8,256,1792]{2,1,0:T(8,128)(2,1)} copy(bf16[8,256,1792]{1,2,0:T(8,128)(2,1)} %all-to-all-done) | data formatting | bytes 14680064 | tf_op jit(solution)/shard_map/all_to_all | solution.py:86
  258.9 11.6 %fusion.22 = f32[1024,1792]{1,0:T(8,128)S(1)} fusion(bf16[2048,1792]{1,0:T(8,128)(2,1)} %bitcast.151, bf16[1,1024,2048]{2,1,0:T(8,128)(2,1)} %all-gather.4.cloned.1.call-done), kind=kOutput, calls=%fused_computation.37 | convolution fusion | flops 7516192768 | bytes 18874368 | tf_op jit(solution)/shard_map/dot_general | solution.py:43
  270.5 3.0 copy-done.5
  275.5 3.5 copy.78
  281.1 10.4 %fusion.95 = (f32[4,1024]{1,0:T(4,128)S(1)}, f32[4,1024,1024]{1,2,0:T(8,128)}) fusion(pred[1024,1024]{0,1:T(8,128)(4,1)S(1)} %iota_compare_fusion, bf16[1024,4,32]{0,2,1:T(8,128)(2,1)S(1)} %get-tuple-element.118, bf16[1024,4,32]{0,2,1:T(8,128)(2,1)S(1)} %get-tuple-element.104, bf16[1024,4,32]{0,2,1:T(8,128)(2,1)S(1)} %get-tuple-element.117, ...), kind=kOutput, calls=%fused_computation.150 | convolution fusion | flops 555746304 | bytes 18890752 | tf_op jit(solution)/shard_map/sub | solution.py:116
  291.6 9.6 fusion.37
  301.2 15.9 %multiply_reduce_fusion = (f32[4,1024]{1,0:T(4,128)S(1)}, f32[4,1024,1024]{1,2,0:T(8,128)}) fusion(f32[4,1024,1024]{1,2,0:T(8,128)} %get-tuple-element.112, f32[4,1024]{1,0:T(4,128)S(1)} %get-tuple-element.111, bf16[1024,4,64]{0,2,1:T(8,128)(2,1)} %bitcast.164, f32[1,1024,3,4,64]{1,4,3,2,0:T(8,128)} %bitcast.148), kind=kOutput, calls=%fused_computation.2 | convolution fusion | flops 549449728 | bytes 34635776 | tf_op jit(solution)/shard_map/sqhd,skhd->shqk/dot_general | solution.py:142
  317.1 8.0 multiply_convert_fusion
  325.2 2.7 fusion.40
  332.5 12.3 %convert_reduce_fusion = (f32[1024]{0:T(1024)}, bf16[1024,1024]{1,0:T(8,128)(2,1)S(1)}) fusion(f32[1024]{0:T(1024)S(1)} %copy-done.35, f32[1024,1792]{1,0:T(8,128)} %copy-done.5, bf16[1024,2048]{1,0:T(8,128)(2,1)} %param.24, bf16[1,1024,2048]{2,1,0:T(8,128)(2,1)} %all-gather.6.cloned.1.call-done), kind=kOutput, calls=%fused_computation.40 | convolution fusion | flops 4319083520 | bytes 14688256 | tf_op jit(solution)/shard_map/dot_general | solution.py:43
  344.8 8.5 convolution_convert_fusion
  353.3 7.0 copy.84
  360.4 12.0 %convert_bitcast_fusion.1 = bf16[1,1024,2048]{2,1,0:T(8,128)(2,1)} fusion(bf16[2048,1792]{1,0:T(8,128)(2,1)} %bitcast.152, bf16[1024,1024]{1,0:T(8,128)(2,1)} %copy-done.42, bf16[1024,768]{1,0:T(8,128)(2,1)S(1)} %copy-done.4), kind=kOutput, calls=%fused_computation.41 | convolution fusion | flops 7525629952 | bytes 15204352 | tf_op jit(solution)/shard_map/dot_general | solution.py:43
  373.4 9.1 fusion.44
  382.5 8.5 fusion.92
  391.0 3.3 fusion.31
  394.6 3.6 fusion.34
  398.2 8.8 fusion.28
  407.0 2.8 pad_maximum_fusion.1
  409.9 38.0 %reduce-scatter.8.cloned.1.call-done = bf16[8,64,1792]{2,0,1:T(8,128)(2,1)} async-done(((bf16[8,256,1792]{2,0,1:T(8,128)(2,1)}), bf16[8,64,1792]{2,0,1:T(8,128)(2,1)}) %reduce-scatter.8.cloned.1.call-update) | async-done | bytes 1835024 | tf_op jit(solution)/shard_map/reduce_scatter | solution.py:174
  448.0 3.0 copy.85
  451.0 4.6 all-to-all-start.1
  456.7 78.3 %reduce-scatter.6.cloned.1.call-done = bf16[1,128,2048]{2,1,0:T(8,128)(2,1)} async-done(((bf16[1,1024,2048]{2,1,0:T(8,128)(2,1)}), bf16[1,128,2048]{2,1,0:T(8,128)(2,1)}) %reduce-scatter.6.cloned.1.call-update) | async-done | bytes 524304 | tf_op jit(solution)/shard_map/reduce_scatter | solution.py:164
  537.1 53.5 %reduce-scatter.4.cloned.1.call-done = bf16[1,128,2048]{2,1,0:T(8,128)(2,1)} async-done(((bf16[1,1024,2048]{2,1,0:T(8,128)(2,1)}), bf16[1,128,2048]{2,1,0:T(8,128)(2,1)}) %reduce-scatter.4.cloned.1.call-update) | async-done | bytes 524304 | tf_op jit(solution)/shard_map/reduce_scatter | solution.py:129
  590.7 3.9 convert_reduce_fusion.4
  594.7 2.2 copy.86
  597.0 5.4 fusion.1
  602.5 38.0 %pmax.7 = f32[32]{0:T(128)S(1)} all-reduce(f32[32]{0:T(128)S(1)} %dynamic_update_slice.11), channel_id=1, replica_groups=mesh['dp'=4,'ctx'=8] {'dp','ctx'}, use_global_device_ids=true, to_apply=%region_22.23 | all-reduce | flops 32 | bytes 256 | tf_op jit(solution)/shard_map/pmax | solution.py:126
  641.3 4.1 convert_multiply_fusion
  645.5 69.2 %all-reduce.4.cloned.1.call-done = bf16[1280,2048]{1,0:T(8,128)(2,1)} async-done(((bf16[1280,2048]{1,0:T(8,128)(2,1)}), bf16[1280,2048]{1,0:T(8,128)(2,1)}) %all-reduce.4.cloned.1.call-update) | async-done | bytes 5242896 | tf_op jit(solution)/shard_map/psum | solution.py:187
  714.7 2.8 slice_convert_fusion.2
  717.5 6.7 slice_convert_fusion
  724.1 120.5 %all-reduce.6.cloned.1.call-done = (f32[2048]{0:T(1024)}, f32[2048]{0:T(1024)}, f32[6144]{0:T(1024)}, f32[2048]{0:T(1024)}, f32[8192]{0:T(1024)}) async-done(((f32[2048]{0:T(1024)}, f32[2048]{0:T(1024)}, f32[6144]{0:T(1024)}, f32[2048]{0:T(1024)}, f32[8192]{0:T(1024)}), (f32[2048]{0:T(1024)}, f32[2048]{0:T(1024)}, f32[6144]{0:T(1024)}, f32[2048]{0:T(1024)}, f32[8192]{0:T(1024)})) %all-reduce.6.cloned.1.call-update) | async-done | bytes 81936 | tf_op jit(solution)/shard_map/psum | solution.py:204
  844.6 82.7 %all-gather.8.cloned.1.call-done = bf16[256,8,1792]{2,1,0:T(8,128)(2,1)} async-done(((bf16[64,8,1792]{2,1,0:T(8,128)(2,1)}), bf16[256,8,1792]{2,1,0:T(8,128)(2,1)}) %all-gather.8.cloned.1.call-update) | async-done | bytes 7340048 | tf_op jit(solution)/shard_map/all_gather | solution.py:178
  927.3 3.8 slice.136
  931.1 5.0 copy.94
  936.1 3.2 slice_convert_fusion.1
  939.3 11.0 %copy.96 = f32[32,8,8,1024]{3,1,2,0:T(8,128)} copy(f32[32,8,8,1024]{3,2,1,0:T(8,128)S(1)} %bitcast.139) | data formatting | bytes 16777216
  951.1 3.3 copy.88
  954.4 6.6 copy.89
  (165 shorter events, 23.6 us)
Async XLA Ops:
  7.2 207.7 %copy-start = (bf16[256,2048]{1,0:T(8,128)(2,1)S(1)}, bf16[256,2048]{1,0:T(8,128)(2,1)}, u32[]{:S(2)}) copy-start(bf16[256,2048]{1,0:T(8,128)(2,1)} %param.20) | copy-start | bytes 3145732
  7.2 207.7 %all-gather.6.cloned.1.call-start = ((), (), s32[]{:S(2)}) async-start(), calls=%async_computation.7 | async-start | bytes 4718592 | tf_op jit(solution)/shard_map/all_gather | solution.py:89
  29.6 6.6 copy-start.1
  29.6 7.8 copy-start.19
  29.6 7.8 copy-start.28
  29.6 9.1 copy-start.37
  29.6 183.3 %copy-start.21 = (f32[6144]{0:T(1024)S(1)}, f32[6144]{0:T(1024)}, u32[]{:S(2)}) copy-start(f32[6144]{0:T(1024)} %param.19) | copy-start | bytes 73732
  29.6 219.4 %all-to-all-start = ((bf16[8,256,1792]{1,2,0:T(8,128)(2,1)}), bf16[8,256,1792]{1,2,0:T(8,128)(2,1)}, u32[]{:S(2)}, u32[]{:S(2)}) async-start(bf16[8,256,1792]{1,2,0:T(8,128)(2,1)} %pad_maximum_fusion), calls=%async_computation | async-start | bytes 14680064 | tf_op jit(solution)/shard_map/all_to_all | solution.py:86
  36.1 222.8 %all-gather.4.cloned.1.call-start = ((), (), s32[]{:S(2)}) async-start(), calls=%async_computation.5 | async-start | bytes 4718592 | tf_op jit(solution)/shard_map/all_gather | solution.py:95
  38.6 409.4 %reduce-scatter.8.cloned.1.call-start = ((), (), s32[]{:S(2)}) async-start(), calls=%async_computation.9 | async-start | bytes 9175040 | tf_op jit(solution)/shard_map/reduce_scatter | solution.py:174
  214.9 76.7 %copy-start.6 = (pred[1024,1024]{0,1:T(8,128)(4,1)}, pred[1024,1024]{0,1:T(8,128)(4,1)S(1)}, u32[]{:S(2)}) copy-start(pred[1024,1024]{0,1:T(8,128)(4,1)S(1)} %iota_compare_fusion) | copy-start | bytes 3145732
  270.5 3.1 copy-start.5
  280.7 10.8 %copy-start.9 = (bf16[1024,4,32]{0,2,1:T(8,128)(2,1)}, bf16[1024,4,32]{0,2,1:T(8,128)(2,1)S(1)}, u32[]{:S(2)}) copy-start(bf16[1024,4,32]{0,2,1:T(8,128)(2,1)S(1)} %get-tuple-element.118) | copy-start | bytes 786436
  280.8 92.2 %copy-start.7 = (bf16[1024,4,32]{0,2,1:T(8,128)(2,1)}, bf16[1024,4,32]{0,2,1:T(8,128)(2,1)S(1)}, u32[]{:S(2)}) copy-start(bf16[1024,4,32]{0,2,1:T(8,128)(2,1)S(1)} %get-tuple-element.117) | copy-start | bytes 786436
  281.1 10.5 %copy-start.12 = (bf16[1024,4,32]{0,2,1:T(8,128)(2,1)}, bf16[1024,4,32]{0,2,1:T(8,128)(2,1)S(1)}, u32[]{:S(2)}) copy-start(bf16[1024,4,32]{0,2,1:T(8,128)(2,1)S(1)} %get-tuple-element.103) | copy-start | bytes 786436
  281.1 10.5 %copy-start.14 = (bf16[1024,4,32]{0,2,1:T(8,128)(2,1)}, bf16[1024,4,32]{0,2,1:T(8,128)(2,1)S(1)}, u32[]{:S(2)}) copy-start(bf16[1024,4,32]{0,2,1:T(8,128)(2,1)S(1)} %get-tuple-element.104) | copy-start | bytes 786436
  301.2 15.9 %slice-start = ((s8[16777216]{0:T(1024)(128)(4,1)}), s8[4194304]{0:T(1024)(128)(4,1)S(1)}, s32[]{:S(2)}) async-start(s8[16777216]{0:T(1024)(128)(4,1)} %bitcast.142), calls=%async_computation.13 | async-start | bytes 8388608
  301.2 15.9 %slice-start.1 = ((s8[16777216]{0:T(1024)(128)(4,1)}), s8[4194304]{0:T(1024)(128)(4,1)S(1)}, s32[]{:S(2)}) async-start(s8[16777216]{0:T(1024)(128)(4,1)} %bitcast.142), calls=%async_computation.14 | async-start | bytes 8388608
  301.2 15.9 %slice-start.2 = ((s8[16777216]{0:T(1024)(128)(4,1)}), s8[4194304]{0:T(1024)(128)(4,1)S(1)}, s32[]{:S(2)}) async-start(s8[16777216]{0:T(1024)(128)(4,1)} %bitcast.142), calls=%async_computation.15 | async-start | bytes 8388608
  301.2 15.9 %slice-start.3 = ((s8[16777216]{0:T(1024)(128)(4,1)}), s8[4194304]{0:T(1024)(128)(4,1)S(1)}, s32[]{:S(2)}) async-start(s8[16777216]{0:T(1024)(128)(4,1)} %bitcast.142), calls=%async_computation.16 | async-start | bytes 8388608
  317.1 8.1 copy-start.13
  332.5 12.3 %copy-start.4 = (bf16[1024,768]{1,0:T(8,128)(2,1)S(1)}, bf16[1024,768]{1,0:T(8,128)(2,1)}, u32[]{:S(2)}) copy-start(bf16[1024,768]{1,0:T(8,128)(2,1)} %copy.83) | copy-start | bytes 4718596
  332.5 12.3 %copy-start.39 = (bf16[1,1024,2048]{2,1,0:T(8,128)(2,1)S(1)}, bf16[1,1024,2048]{2,1,0:T(8,128)(2,1)}, u32[]{:S(2)}) copy-start(bf16[1,1024,2048]{2,1,0:T(8,128)(2,1)} %all-gather.4.cloned.1.call-done) | copy-start | bytes 12582916
  344.8 8.5 copy-start.42
  360.3 174.7 %reduce-scatter.6.cloned.1.call-start = ((), (), s32[]{:S(2)}) async-start(), calls=%async_computation.8 | async-start | bytes 4718592 | tf_op jit(solution)/shard_map/reduce_scatter | solution.py:164
  372.4 218.2 %reduce-scatter.4.cloned.1.call-start = ((), (), s32[]{:S(2)}) async-start(), calls=%async_computation.6 | async-start | bytes 4718592 | tf_op jit(solution)/shard_map/reduce_scatter | solution.py:129
  394.4 320.3 %all-reduce.4.cloned.1.call-start = ((), (), s32[]{:S(2)}) async-start(), calls=%async_computation.11 | async-start | bytes 10485760 | tf_op jit(solution)/shard_map/psum | solution.py:187
  394.6 3.6 copy-start.38
  409.9 46.6 %copy-start.36 = (f32[1024]{0:T(1024)S(1)}, f32[1024]{0:T(1024)}, u32[]{:S(2)}) copy-start(f32[1024]{0:T(1024)} %get-tuple-element.115) | copy-start | bytes 12292
  409.9 125.1 %copy-start.2 = (bf16[1,128,2048]{2,1,0:T(8,128)(2,1)S(1)}, bf16[1,128,2048]{2,1,0:T(8,128)(2,1)}, u32[]{:S(2)}) copy-start(bf16[1,128,2048]{2,1,0:T(8,128)(2,1)} %param.14) | copy-start | bytes 1572868
  409.9 125.1 %copy-start.20 = (f32[2048]{0:T(1024)S(1)}, f32[2048]{0:T(1024)}, u32[]{:S(2)}) copy-start(f32[2048]{0:T(1024)} %param.16) | copy-start | bytes 24580
  409.9 125.1 %copy-start.27 = (f32[128]{0:T(128)S(1)}, f32[128]{0:T(128)}, u32[]{:S(2)}) copy-start(f32[128]{0:T(128)} %copy-done.26) | copy-start | bytes 1540
  409.9 125.1 %copy-start.34 = (f32[128]{0:T(128)S(1)}, f32[128]{0:T(128)}, u32[]{:S(2)}) copy-start(f32[128]{0:T(128)} %copy-done.33) | copy-start | bytes 1540
  409.9 180.8 %copy-start.29 = (f32[2048]{0:T(1024)S(1)}, f32[2048]{0:T(1024)}, u32[]{:S(2)}) copy-start(f32[2048]{0:T(1024)} %param.25) | copy-start | bytes 24580
  409.9 180.7 %copy-start.30 = (f32[2048]{0:T(1024)S(1)}, f32[2048]{0:T(1024)}, u32[]{:S(2)}) copy-start(f32[2048]{0:T(1024)} %param.21) | copy-start | bytes 24580
  451.0 143.6 %all-to-all-start.1 = ((bf16[8,64,1792]{2,1,0:T(8,128)(2,1)}), bf16[8,64,1792]{2,1,0:T(8,128)(2,1)S(1)}, u32[]{:S(2)}, u32[]{:S(2)}) async-start(bf16[8,64,1792]{2,1,0:T(8,128)(2,1)} %copy.85), calls=%async_computation.4 | async-start | bytes 3670016 | tf_op jit(solution)/shard_map/all_to_all | solution.py:177
  455.6 389.0 %all-reduce.6.cloned.1.call-start = ((), (), s32[]{:S(2)}) async-start(), calls=%async_computation.12 | async-start | bytes 163840 | tf_op jit(solution)/shard_map/psum | solution.py:204
  456.7 137.9 %copy-start.18 = (f32[8192]{0:T(1024)}, f32[8192]{0:T(1024)S(1)}, u32[]{:S(2)}) copy-start(f32[8192]{0:T(1024)S(1)} %dynamic_update_slice.10) | copy-start | bytes 98308
  594.6 332.7 %all-gather.8.cloned.1.call-start = ((), (), s32[]{:S(2)}) async-start(), calls=%async_computation.10 | async-start | bytes 9175040 | tf_op jit(solution)/shard_map/all_gather | solution.py:178
  597.0 43.6 %copy-start.40 = (s32[32]{0:T(128)S(1)}, s32[32]{0:T(128)}, u32[]{:S(2)}) copy-start(s32[32]{0:T(128)} %param.26) | copy-start | bytes 388
  597.0 43.7 %copy-start.22 = (f32[6144]{0:T(1024)S(1)}, f32[6144]{0:T(1024)}, u32[]{:S(2)}) copy-start(f32[6144]{0:T(1024)} %param.19) | copy-start | bytes 73732
  640.5 76.9 %copy-start.41 = (f32[32]{0:T(128)}, f32[32]{0:T(128)S(1)}, u32[]{:S(2)}) copy-start(f32[32]{0:T(128)S(1)} %pmax.7) | copy-start | bytes 388
  939.3 11.0 %copy-start.3 = (bf16[256,8,768]{0,2,1:T(8,128)(2,1)S(1)}, bf16[256,8,768]{0,2,1:T(8,128)(2,1)}, u32[]{:S(2)}) copy-start(bf16[256,8,768]{0,2,1:T(8,128)(2,1)} %copy.94) | copy-start | bytes 9437188
  954.4 6.6 copy-start.24
  954.4 7.2 copy-start.32
  954.4 7.8 copy-start.31
  954.4 8.4 copy-start.25
  954.4 9.6 copy-start.23
  (9 other events, 15.6 us)
Sparse Core Ops, SparseCore 0:
  9.6 67.6 all-gather.5
  79.5 135.0 all-gather.3
  360.5 87.4 reduce-scatter.7
  450.7 84.2 reduce-scatter.5
  537.7 52.9 reduce-scatter.3
  594.4 120.2 all-reduce.3
  722.2 122.3 all-reduce.5
  847.1 80.2 all-gather.7
where the time goes:
time: 976 us; the launch traced here: 972 us
  waiting for transfers between devices  473 us (48%)
  blocking collectives  212 us (22%)
  matrix products  128 us (13%)
  local copies, waits for them, and re-layouts  84.9 us (9%)
  other arithmetic  47 us (5%)
  between operations  15 us (2%)
  starting transfers between devices  12 us (1%)
    all_gather x1, blocking collectives, per_device(): all_positions = lax.all_gather(positions, 'ctx', axis=1, tiled=True)  174 us
    psum x1, waiting for transfers between devices, per_device(): lax.psum((gain_part, shift_part, qkv_bias_part, out_bias_grad, up_bias_pa...  121 us
    all_gather x1, waiting for transfers between devices, per_device(): lax.all_gather(in_quarter.transpose(1, 0, 2), 'dp', axis=0, tiled=True)  82.7 us
    reduce_scatter x1, waiting for transfers between devices, per_device(): lax.psum_scatter(hidden_part.astype(BF16).reshape(seqs, length, width), '...  78.3 us
    dot_general x9, matrix products, dot(): lax.dot_general(left, right, ((contract[:1], contract[1:]), ((), ())), pr...  73.4 us
    psum x1, waiting for transfers between devices, per_device(): lax.psum(jnp.concatenate([dense_grad, down_grad], axis=0).astype(BF16), '...  69.2 us
    reduce_scatter x1, waiting for transfers between devices, per_device(): lax.psum_scatter(branch.astype(BF16).reshape(seqs, length, width), 'ctx',...  53.5 us
    unnamed x108, local copies, waits for them, and re-layouts  42.9 us
  transfers between devices with their start and end apart: 10, of which 7 were waited for; matrix products, arithmetic and copies ran while one was open for 12% of the time, Pallas kernels for 0%

commit v1 on v0

--- a/solution.py
+++ b/solution.py
@@ -175,7 +175,17 @@
         in_grad.reshape(parts, own_rows, 3 * own + own_ff), "dp", scatter_dimension=1, tiled=True
     )
     in_quarter = lax.all_to_all(in_quarter, "ctx", split_axis=0, concat_axis=0, tiled=True)
-    in_rows = lax.all_gather(in_quarter.transpose(1, 0, 2), "dp", axis=0, tiled=True)
+    shard = in_quarter.transpose(1, 0, 2)
+    ways = lax.axis_size("dp")
+    up = [(d, (d + 1) % ways) for d in range(ways)]
+    down = [(d, (d - 1) % ways) for d in range(ways)]
+    earlier, later = ([shard], [shard])
+    for _ in range(ways // 2):
+        earlier.append(lax.ppermute(earlier[-1], "dp", up))
+    for _ in range((ways - 1) // 2):
+        later.append(lax.ppermute(later[-1], "dp", down))
+    line = jnp.concatenate([*earlier[::-1], *later[1:]], axis=0)
+    in_rows = jnp.roll(line, (lax.axis_index("dp") - ways // 2) * shard.shape[0], axis=0)
     qkv_grad = (
         in_rows[:, :, : 3 * own]
         .reshape(own_rows, parts, 3, own)

time: 976 us -> 931 us (0.954)
  waiting for transfers between devices: 473 us -> 316 us
  blocking collectives: 212 us -> 265 us
  local copies, waits for them, and re-layouts: 84.9 us -> 136 us
    all_gather x1 -> x0, waiting for transfers between devices: 82.7 us -> none  [per_device(): lax.all_gather(in_quarter.transpose(1, 0, 2), 'dp', axis=0, tiled=True)]
    psum x1, waiting for transfers between devices: 69.2 us -> 0.01 us  [per_device(): lax.psum(jnp.concatenate([dense_grad, down_grad], axis=0).astype(BF16), '...]
    pmax x1, blocking collectives: 38 us -> 90.4 us  [per_device(): head_maxima = lax.pmax(slots, ('dp', 'ctx'))]
    reduce_scatter x1, waiting for transfers between devices: 78.3 us -> 34.9 us  [per_device(): lax.psum_scatter(hidden_part.astype(BF16).reshape(seqs, length, width), '...]
    all_to_all x1, waiting for transfers between devices: 0.01 us -> 43.4 us  [per_device(): lax.all_to_all(in_quarter, 'ctx', split_axis=0, concat_axis=0, tiled=True)]
    concatenate x0 -> x1, local copies, waits for them, and re-layouts: none -> 33.8 us  [per_device(): jnp.roll(line, (lax.axis_index('dp') - ways // 2) * shard.shape[0], axis=0)]
    ppermute x0 -> x3, local copies, waits for them, and re-layouts: none -> 14.8 us  [the longest x2 9.87 us: per_device(): earlier.append(lax.ppermute(earlier[-1], 'dp', up))]
    unnamed x108 -> x101, local copies, waits for them, and re-layouts: 42.9 us -> 36 us
  transfers between devices with their start and end apart: 10 -> 12, of which waited for: 7 -> 6; matrix products, arithmetic and copies ran while one was open for 12% -> 14% of each run, Pallas kernels for 0% -> 0%
where the time goes in v1:
time: 931 us; the launch traced here: 923 us
  waiting for transfers between devices  316 us (34%)
  blocking collectives  265 us (28%)
  local copies, waits for them, and re-layouts  136 us (15%)
  matrix products  128 us (14%)
  other arithmetic  48.2 us (5%)
  starting transfers between devices  15.7 us (2%)
  between operations  15 us (2%)
    all_gather x1, blocking collectives, per_device(): all_positions = lax.all_gather(positions, 'ctx', axis=1, tiled=True)  174 us
    psum x1, waiting for transfers between devices, per_device(): lax.psum((gain_part, shift_part, qkv_bias_part, out_bias_grad, up_bias_pa...  121 us
    pmax x1, blocking collectives, per_device(): head_maxima = lax.pmax(slots, ('dp', 'ctx'))  90.4 us
    dot_general x9, matrix products, dot(): lax.dot_general(left, right, ((contract[:1], contract[1:]), ((), ())), pr...  72.5 us
    reduce_scatter x1, waiting for transfers between devices, per_device(): lax.psum_scatter(branch.astype(BF16).reshape(seqs, length, width), 'ctx',...  48.8 us
    all_to_all x1, waiting for transfers between devices, per_device(): lax.all_to_all(in_quarter, 'ctx', split_axis=0, concat_axis=0, tiled=True)  43.4 us
    reduce_scatter x1, waiting for transfers between devices, per_device(): lax.psum_scatter(in_grad.reshape(parts, own_rows, 3 * own + own_ff), 'dp'...  36.4 us
    unnamed x101, local copies, waits for them, and re-layouts  36 us
  transfers between devices with their start and end apart: 12, of which 6 were waited for; matrix products, arithmetic and copies ran while one was open for 14% of the time, Pallas kernels for 0%

profile of v1, /device:TPU:0, one launch (start us, length us, event | category | flops | bytes accessed | tf_op | source)
XLA Modules:
  0.0 923.1 jit_solution(4840171339477497677)
XLA Ops:
  7.9 4.6 copy.74
  12.6 3.9 copy.75
  16.4 6.4 copy.76
  22.9 6.7 pad_maximum_fusion
  29.6 6.5 all-to-all-start
  38.7 174.2 %all_gather.10 = s32[1,1024]{1,0:T(1,128)S(1)} all-gather(s32[1,128]{1,0:T(1,128)S(1)} %copy-done.34), channel_id=1, replica_groups=mesh['dp'=4,'ctx'=8] {'ctx'}, dimensions={1}, use_global_device_ids=true | all-gather | bytes 4608 | tf_op jit(solution)/shard_map/all_gather | solution.py:98
  214.3 4.6 fusion.47
  218.9 30.1 %all-to-all-done = bf16[8,256,1792]{1,2,0:T(8,128)(2,1)} async-done(((bf16[8,256,1792]{1,2,0:T(8,128)(2,1)}), bf16[8,256,1792]{1,2,0:T(8,128)(2,1)}, u32[]{:S(2)}, u32[]{:S(2)}) %all-to-all-start) | async-done | bytes 7340064 | tf_op jit(solution)/shard_map/all_to_all | solution.py:86
  248.9 10.1 %copy.77 = bf16[8,256,1792]{2,1,0:T(8,128)(2,1)} copy(bf16[8,256,1792]{1,2,0:T(8,128)(2,1)} %all-to-all-done) | data formatting | bytes 14680064 | tf_op jit(solution)/shard_map/all_to_all | solution.py:86
  259.0 11.6 %fusion.22 = f32[1024,1792]{1,0:T(8,128)S(1)} fusion(bf16[2048,1792]{1,0:T(8,128)(2,1)} %bitcast.155, bf16[1,1024,2048]{2,1,0:T(8,128)(2,1)} %all-gather.3.cloned.1.call-done), kind=kOutput, calls=%fused_computation.37 | convolution fusion | flops 7516192768 | bytes 18874368 | tf_op jit(solution)/shard_map/dot_general | solution.py:43
  270.7 3.0 copy-done.4
  275.6 3.5 copy.78
  281.3 9.9 %fusion.95 = (f32[4,1024]{1,0:T(4,128)S(1)}, f32[4,1024,1024]{1,2,0:T(8,128)}) fusion(pred[1024,1024]{0,1:T(8,128)(4,1)S(1)} %iota_compare_fusion, bf16[1024,4,32]{0,2,1:T(8,128)(2,1)S(1)} %get-tuple-element.118, bf16[1024,4,32]{0,2,1:T(8,128)(2,1)S(1)} %get-tuple-element.104, bf16[1024,4,32]{0,2,1:T(8,128)(2,1)S(1)} %get-tuple-element.117, ...), kind=kOutput, calls=%fused_computation.152 | convolution fusion | flops 555746304 | bytes 18890752 | tf_op jit(solution)/shard_map/sub | solution.py:116
  291.3 15.8 %multiply_reduce_fusion = (f32[4,1024]{1,0:T(4,128)S(1)}, f32[4,1024,1024]{1,2,0:T(8,128)}) fusion(f32[4,1024,1024]{1,2,0:T(8,128)} %get-tuple-element.112, f32[4,1024]{1,0:T(4,128)S(1)} %get-tuple-element.111, bf16[1024,4,64]{0,2,1:T(8,128)(2,1)} %bitcast.166, f32[1,1024,3,4,64]{1,4,3,2,0:T(8,128)} %bitcast.153), kind=kOutput, calls=%fused_computation.2 | convolution fusion | flops 549449728 | bytes 34635776 | tf_op jit(solution)/shard_map/sqhd,skhd->shqk/dot_general | solution.py:142
  307.2 8.2 multiply_convert_fusion
  319.7 10.2 %fusion.37 = bf16[1,1024,1,4,64]{1,4,3,2,0:T(8,128)(2,1)} fusion(bf16[1024,4,64]{0,2,1:T(8,128)(2,1)} %bitcast.167, f32[4,1024]{1,0:T(4,128)S(1)} %get-tuple-element.111, pred[1024,1024]{0,1:T(8,128)(4,1)} %copy-done.5, bf16[1024,4,32]{0,2,1:T(8,128)(2,1)} %copy-done.8, bf16[1024,4,32]{0,2,1:T(8,128)(2,1)} %copy-done.13, ...), kind=kOutput, calls=%fused_computation.62 | convolution fusion | flops 1096815616 | bytes 3162112 | tf_op jit(solution)/shard_map/shqk,sqhd->skhd/dot_general | solution.py:141
  333.1 11.7 %convert_reduce_fusion = (f32[1024]{0:T(1024)S(1)}, bf16[1024,1024]{1,0:T(8,128)(2,1)S(1)}) fusion(f32[1024]{0:T(1024)S(1)} %dynamic_slice.11, f32[1024,1792]{1,0:T(8,128)} %copy-done.4, bf16[1024,2048]{1,0:T(8,128)(2,1)} %param.24, bf16[1,1024,2048]{2,1,0:T(8,128)(2,1)} %all-gather.5.cloned.1.call-done), kind=kOutput, calls=%fused_computation.40 | convolution fusion | flops 4319083520 | bytes 14688256 | tf_op jit(solution)/shard_map/dot_general | solution.py:43
  344.8 8.3 convolution_convert_fusion
  353.2 7.0 copy.84
  361.3 10.0 %fusion.44 = bf16[4,64,1024]{2,1,0:T(8,128)(2,1)} fusion(f32[1,1024,3,4,64]{1,4,3,2,0:T(8,128)} %bitcast.154, f32[4,1024]{1,0:T(4,128)S(1)} %get-tuple-element.111, pred[1024,1024]{0,1:T(8,128)(4,1)} %copy-done.5, bf16[1024,4,32]{0,2,1:T(8,128)(2,1)S(1)} %copy-done.10, bf16[1024,4,32]{0,2,1:T(8,128)(2,1)} %copy-done.13, ...), kind=kOutput, calls=%fused_computation.71 | convolution fusion | flops 1097077760 | bytes 3162112 | tf_op jit(solution)/shard_map/shqk,skhd->sqhd/dot_general | solution.py:120
  371.3 3.7 fusion.34
  375.1 8.5 fusion.28
  386.7 12.5 %convert_bitcast_fusion.1 = bf16[1,1024,2048]{2,1,0:T(8,128)(2,1)} fusion(bf16[2048,1792]{1,0:T(8,128)(2,1)} %bitcast.156, bf16[1024,1024]{1,0:T(8,128)(2,1)} %copy-done.39, bf16[1024,768]{1,0:T(8,128)(2,1)S(1)} %copy-done.3), kind=kOutput, calls=%fused_computation.41 | convolution fusion | flops 7525629952 | bytes 15204352 | tf_op jit(solution)/shard_map/dot_general | solution.py:43
  399.3 8.1 fusion.92
  407.4 3.3 fusion.31
  410.8 36.4 %reduce-scatter.8.cloned.1.call-done = bf16[8,64,1792]{2,0,1:T(8,128)(2,1)} async-done(((bf16[8,256,1792]{2,0,1:T(8,128)(2,1)}), bf16[8,64,1792]{2,0,1:T(8,128)(2,1)}) %reduce-scatter.8.cloned.1.call-update) | async-done | bytes 1835024 | tf_op jit(solution)/shard_map/reduce_scatter | solution.py:174
  447.2 3.0 copy.85
  450.2 4.6 all-to-all-start.1
  454.9 43.4 %all-to-all-done.1 = bf16[8,64,1792]{2,1,0:T(8,128)(2,1)S(1)} async-done(((bf16[8,64,1792]{2,1,0:T(8,128)(2,1)}), bf16[8,64,1792]{2,1,0:T(8,128)(2,1)S(1)}, u32[]{:S(2)}, u32[]{:S(2)}) %all-to-all-start.1) | async-done | bytes 1835040 | tf_op jit(solution)/shard_map/all_to_all | solution.py:177
  501.8 4.9 fusion.1
  506.9 90.4 %pmax.7 = f32[32]{0:T(128)S(1)} all-reduce(f32[32]{0:T(128)S(1)} %dynamic_update_slice.11), channel_id=1, replica_groups=mesh['dp'=4,'ctx'=8] {'dp','ctx'}, use_global_device_ids=true, to_apply=%region_22.23 | all-reduce | flops 32 | bytes 256 | tf_op jit(solution)/shard_map/pmax | solution.py:126
  599.2 4.1 convert_multiply_fusion
  605.8 6.7 slice_convert_fusion
  612.5 34.9 %reduce-scatter.6.cloned.1.call-done = bf16[1,128,2048]{2,1,0:T(8,128)(2,1)} async-done(((bf16[1,1024,2048]{2,1,0:T(8,128)(2,1)}), bf16[1,128,2048]{2,1,0:T(8,128)(2,1)}) %reduce-scatter.6.cloned.1.call-update) | async-done | bytes 524304 | tf_op jit(solution)/shard_map/reduce_scatter | solution.py:164
  649.5 48.8 %reduce-scatter.4.cloned.1.call-done = bf16[1,128,2048]{2,1,0:T(8,128)(2,1)} async-done(((bf16[1,1024,2048]{2,1,0:T(8,128)(2,1)}), bf16[1,128,2048]{2,1,0:T(8,128)(2,1)}) %reduce-scatter.4.cloned.1.call-update) | async-done | bytes 524304 | tf_op jit(solution)/shard_map/reduce_scatter | solution.py:129
  698.2 3.9 convert_reduce_fusion.4
  705.0 121.4 %all-reduce.6.cloned.1.call-done = (f32[2048]{0:T(1024)}, f32[2048]{0:T(1024)}, f32[6144]{0:T(1024)}, f32[2048]{0:T(1024)}, f32[8192]{0:T(1024)}) async-done(((f32[2048]{0:T(1024)}, f32[2048]{0:T(1024)}, f32[6144]{0:T(1024)}, f32[2048]{0:T(1024)}, f32[8192]{0:T(1024)}), (f32[2048]{0:T(1024)}, f32[2048]{0:T(1024)}, f32[6144]{0:T(1024)}, f32[2048]{0:T(1024)}, f32[8192]{0:T(1024)})) %all-reduce.6.cloned.1.call-update) | async-done | bytes 81936 | tf_op jit(solution)/shard_map/psum | solution.py:214
  826.4 3.0 copy.86
  829.4 4.9 copy.90
  834.3 5.0 copy.91
  839.3 4.9 copy.89
  844.2 33.8 %concatenate.102 = bf16[512,8,1792]{0,2,1:T(8,128)(2,1)} concatenate(bf16[64,8,1792]{0,2,1:T(8,128)(2,1)} %copy.89, bf16[64,8,1792]{0,2,1:T(8,128)(2,1)} %copy.90, bf16[64,8,1792]{0,2,1:T(8,128)(2,1)} %bitcast.142, bf16[64,8,1792]{0,2,1:T(8,128)(2,1)} %copy.91, bf16[64,8,1792]{0,2,1:T(8,128)(2,1)} %copy.89, bf16[64,8,1792]{0,2,1:T(8,128)(2,1)} %copy.90, ...), dimensions={0} | concatenate | bytes 29360128 | tf_op jit(solution)/shard_map/jit(_roll_dynamic)/concatenate | solution.py:188
  878.0 4.0 constant_dynamic-slice_fusion
  882.7 3.4 copy.95
  886.1 6.6 copy.96
  892.6 6.6 constant_dynamic-slice_fusion.1
  899.2 4.2 bitcast_convert_fusion
  903.5 9.0 copy.97
  (167 shorter events, 37.7 us)
Async XLA Ops:
  7.2 207.1 %copy-start = (bf16[256,2048]{1,0:T(8,128)(2,1)S(1)}, bf16[256,2048]{1,0:T(8,128)(2,1)}, u32[]{:S(2)}) copy-start(bf16[256,2048]{1,0:T(8,128)(2,1)} %param.20) | copy-start | bytes 3145732
  7.2 207.1 %all-gather.5.cloned.1.call-start = ((), (), s32[]{:S(2)}) async-start(), calls=%async_computation.7 | async-start | bytes 4718592 | tf_op jit(solution)/shard_map/all_gather | solution.py:89
  29.6 6.6 copy-start.1
  29.6 7.8 copy-start.18
  29.6 7.8 copy-start.27
  29.6 9.1 copy-start.20
  29.6 9.1 copy-start.34
  29.6 219.4 %all-to-all-start = ((bf16[8,256,1792]{1,2,0:T(8,128)(2,1)}), bf16[8,256,1792]{1,2,0:T(8,128)(2,1)}, u32[]{:S(2)}, u32[]{:S(2)}) async-start(bf16[8,256,1792]{1,2,0:T(8,128)(2,1)} %pad_maximum_fusion), calls=%async_computation | async-start | bytes 14680064 | tf_op jit(solution)/shard_map/all_to_all | solution.py:86
  36.1 222.9 %all-gather.3.cloned.1.call-start = ((), (), s32[]{:S(2)}) async-start(), calls=%async_computation.5 | async-start | bytes 4718592 | tf_op jit(solution)/shard_map/all_gather | solution.py:95
  38.6 408.6 %reduce-scatter.8.cloned.1.call-start = ((), (), s32[]{:S(2)}) async-start(), calls=%async_computation.9 | async-start | bytes 9175040 | tf_op jit(solution)/shard_map/reduce_scatter | solution.py:174
  214.2 67.1 %copy-start.5 = (pred[1024,1024]{0,1:T(8,128)(4,1)}, pred[1024,1024]{0,1:T(8,128)(4,1)S(1)}, u32[]{:S(2)}) copy-start(pred[1024,1024]{0,1:T(8,128)(4,1)S(1)} %iota_compare_fusion) | copy-start | bytes 3145732
  270.7 3.1 copy-start.4
  281.0 10.2 %copy-start.8 = (bf16[1024,4,32]{0,2,1:T(8,128)(2,1)}, bf16[1024,4,32]{0,2,1:T(8,128)(2,1)S(1)}, u32[]{:S(2)}) copy-start(bf16[1024,4,32]{0,2,1:T(8,128)(2,1)S(1)} %get-tuple-element.118) | copy-start | bytes 786436
  281.0 34.4 %copy-start.6 = (bf16[1024,4,32]{0,2,1:T(8,128)(2,1)}, bf16[1024,4,32]{0,2,1:T(8,128)(2,1)S(1)}, u32[]{:S(2)}) copy-start(bf16[1024,4,32]{0,2,1:T(8,128)(2,1)S(1)} %get-tuple-element.117) | copy-start | bytes 786436
  281.3 10.0 %copy-start.13 = (bf16[1024,4,32]{0,2,1:T(8,128)(2,1)}, bf16[1024,4,32]{0,2,1:T(8,128)(2,1)S(1)}, u32[]{:S(2)}) copy-start(bf16[1024,4,32]{0,2,1:T(8,128)(2,1)S(1)} %get-tuple-element.104) | copy-start | bytes 786436
  281.3 34.1 %copy-start.11 = (bf16[1024,4,32]{0,2,1:T(8,128)(2,1)}, bf16[1024,4,32]{0,2,1:T(8,128)(2,1)S(1)}, u32[]{:S(2)}) copy-start(bf16[1024,4,32]{0,2,1:T(8,128)(2,1)S(1)} %get-tuple-element.103) | copy-start | bytes 786436
  291.2 15.9 %slice-start = ((s8[16777216]{0:T(1024)(128)(4,1)}), s8[4194304]{0:T(1024)(128)(4,1)S(1)}, s32[]{:S(2)}) async-start(s8[16777216]{0:T(1024)(128)(4,1)} %bitcast.146), calls=%async_computation.12 | async-start | bytes 8388608
  291.2 15.9 %slice-start.1 = ((s8[16777216]{0:T(1024)(128)(4,1)}), s8[4194304]{0:T(1024)(128)(4,1)S(1)}, s32[]{:S(2)}) async-start(s8[16777216]{0:T(1024)(128)(4,1)} %bitcast.146), calls=%async_computation.13 | async-start | bytes 8388608
  291.3 15.9 %slice-start.2 = ((s8[16777216]{0:T(1024)(128)(4,1)}), s8[4194304]{0:T(1024)(128)(4,1)S(1)}, s32[]{:S(2)}) async-start(s8[16777216]{0:T(1024)(128)(4,1)} %bitcast.146), calls=%async_computation.14 | async-start | bytes 8388608
  291.3 15.9 %slice-start.3 = ((s8[16777216]{0:T(1024)(128)(4,1)}), s8[4194304]{0:T(1024)(128)(4,1)S(1)}, s32[]{:S(2)}) async-start(s8[16777216]{0:T(1024)(128)(4,1)} %bitcast.146), calls=%async_computation.15 | async-start | bytes 8388608
  333.0 11.8 %copy-start.3 = (bf16[1024,768]{1,0:T(8,128)(2,1)S(1)}, bf16[1024,768]{1,0:T(8,128)(2,1)}, u32[]{:S(2)}) copy-start(bf16[1024,768]{1,0:T(8,128)(2,1)} %copy.83) | copy-start | bytes 4718596
  333.0 11.8 %copy-start.36 = (bf16[1,1024,2048]{2,1,0:T(8,128)(2,1)S(1)}, bf16[1,1024,2048]{2,1,0:T(8,128)(2,1)}, u32[]{:S(2)}) copy-start(bf16[1,1024,2048]{2,1,0:T(8,128)(2,1)} %all-gather.3.cloned.1.call-done) | copy-start | bytes 12582916
  344.8 8.4 copy-start.39
  360.2 245.6 %all-reduce.4.cloned.1.call-start = ((), (), s32[]{:S(2)}) async-start(), calls=%async_computation.10 | async-start | bytes 10485760 | tf_op jit(solution)/shard_map/psum | solution.py:197
  371.3 3.8 copy-start.35
  386.5 260.9 %reduce-scatter.6.cloned.1.call-start = ((), (), s32[]{:S(2)}) async-start(), calls=%async_computation.8 | async-start | bytes 4718592 | tf_op jit(solution)/shard_map/reduce_scatter | solution.py:164
  399.2 8.2 copy-start.15
  399.3 299.0 %reduce-scatter.4.cloned.1.call-start = ((), (), s32[]{:S(2)}) async-start(), calls=%async_computation.6 | async-start | bytes 4718592 | tf_op jit(solution)/shard_map/reduce_scatter | solution.py:129
  450.2 48.1 %all-to-all-start.1 = ((bf16[8,64,1792]{2,1,0:T(8,128)(2,1)}), bf16[8,64,1792]{2,1,0:T(8,128)(2,1)S(1)}, u32[]{:S(2)}, u32[]{:S(2)}) async-start(bf16[8,64,1792]{2,1,0:T(8,128)(2,1)} %copy.85), calls=%async_computation.4 | async-start | bytes 3670016 | tf_op jit(solution)/shard_map/all_to_all | solution.py:177
  454.8 371.6 %all-reduce.6.cloned.1.call-start = ((), (), s32[]{:S(2)}) async-start(), calls=%async_computation.11 | async-start | bytes 163840 | tf_op jit(solution)/shard_map/psum | solution.py:214
  500.5 96.8 %copy-start.37 = (s32[32]{0:T(128)S(1)}, s32[32]{0:T(128)}, u32[]{:S(2)}) copy-start(s32[32]{0:T(128)} %param.26) | copy-start | bytes 388
  500.5 98.1 %copy-start.21 = (f32[6144]{0:T(1024)S(1)}, f32[6144]{0:T(1024)}, u32[]{:S(2)}) copy-start(f32[6144]{0:T(1024)} %param.19) | copy-start | bytes 73732
  500.5 105.3 %collective-permute-start = (bf16[64,8,1792]{2,1,0:T(8,128)(2,1)}, bf16[64,8,1792]{2,1,0:T(8,128)(2,1)}, u32[]{:S(2)}, u32[]{:S(2)}) collective-permute-start(bf16[64,8,1792]{2,1,0:T(8,128)(2,1)} %copy.87), channel_id=1, source_target_pairs={{0,8},{8,16},{16,24},{24,0},{1,9},{9,17},{17,25},{25,1},{2,10},{10... | collective-permute-start | bytes 5505032 | tf_op jit(solution)/shard_map/ppermute | solution.py:184
  597.3 15.2 %copy-start.38 = (f32[32]{0:T(128)}, f32[32]{0:T(128)S(1)}, u32[]{:S(2)}) copy-start(f32[32]{0:T(128)S(1)} %pmax.7) | copy-start | bytes 388
  598.6 13.8 %copy-start.17 = (f32[8192]{0:T(1024)}, f32[8192]{0:T(1024)S(1)}, u32[]{:S(2)}) copy-start(f32[8192]{0:T(1024)S(1)} %dynamic_update_slice.10) | copy-start | bytes 98308
  603.4 44.0 %copy-start.2 = (bf16[1,128,2048]{2,1,0:T(8,128)(2,1)S(1)}, bf16[1,128,2048]{2,1,0:T(8,128)(2,1)}, u32[]{:S(2)}) copy-start(bf16[1,128,2048]{2,1,0:T(8,128)(2,1)} %param.14) | copy-start | bytes 1572868
  603.4 44.0 %copy-start.19 = (f32[2048]{0:T(1024)S(1)}, f32[2048]{0:T(1024)}, u32[]{:S(2)}) copy-start(f32[2048]{0:T(1024)} %param.16) | copy-start | bytes 24580
  603.4 44.0 %copy-start.26 = (f32[128]{0:T(128)S(1)}, f32[128]{0:T(128)}, u32[]{:S(2)}) copy-start(f32[128]{0:T(128)} %copy-done.25) | copy-start | bytes 1540
  603.4 44.0 %copy-start.33 = (f32[128]{0:T(128)S(1)}, f32[128]{0:T(128)}, u32[]{:S(2)}) copy-start(f32[128]{0:T(128)} %copy-done.32) | copy-start | bytes 1540
  603.4 94.9 %copy-start.28 = (f32[2048]{0:T(1024)S(1)}, f32[2048]{0:T(1024)}, u32[]{:S(2)}) copy-start(f32[2048]{0:T(1024)} %param.25) | copy-start | bytes 24580
  603.4 94.9 %copy-start.29 = (f32[2048]{0:T(1024)S(1)}, f32[2048]{0:T(1024)}, u32[]{:S(2)}) copy-start(f32[2048]{0:T(1024)} %param.21) | copy-start | bytes 24580
  603.4 230.9 %collective-permute-start.2 = (bf16[64,8,1792]{2,1,0:T(8,128)(2,1)}, bf16[64,8,1792]{2,1,0:T(8,128)(2,1)}, u32[]{:S(2)}, u32[]{:S(2)}) collective-permute-start(bf16[64,8,1792]{2,1,0:T(8,128)(2,1)} %copy.87), channel_id=1, source_target_pairs={{0,24},{8,0},{16,8},{24,16},{1,25},{9,1},{17,9},{25,17},{2,26},{10... | collective-permute-start | bytes 5505032 | tf_op jit(solution)/shard_map/ppermute | solution.py:186
  605.8 233.5 %collective-permute-start.1 = (bf16[64,8,1792]{2,1,0:T(8,128)(2,1)}, bf16[64,8,1792]{2,1,0:T(8,128)(2,1)}, u32[]{:S(2)}, u32[]{:S(2)}) collective-permute-start(bf16[64,8,1792]{2,1,0:T(8,128)(2,1)} %collective-permute-done), channel_id=1, source_target_pairs={{0,8},{8,16},{16,24},{24,0},{1,9},{9,17},{17,25},{25,1},{2,10},{10... | collective-permute-start | bytes 5505032 | tf_op jit(solution)/shard_map/ppermute | solution.py:184
  903.4 9.0 copy-start.23
  903.4 9.6 %copy-start.31 = (f32[2048]{0:T(1024)S(1)}, f32[2048]{0:T(1024)}, u32[]{:S(2)}) copy-start(f32[2048]{0:T(1024)} %get-tuple-element.155) | copy-start | bytes 24580
  903.4 10.2 %copy-start.30 = (f32[2048]{0:T(1024)S(1)}, f32[2048]{0:T(1024)}, u32[]{:S(2)}) copy-start(f32[2048]{0:T(1024)} %get-tuple-element.156) | copy-start | bytes 24580
  903.4 10.8 %copy-start.24 = (f32[6144]{0:T(1024)S(1)}, f32[6144]{0:T(1024)}, u32[]{:S(2)}) copy-start(f32[6144]{0:T(1024)} %get-tuple-element.158) | copy-start | bytes 73732
  903.4 12.0 %copy-start.22 = (f32[8192]{0:T(1024)S(1)}, f32[8192]{0:T(1024)}, u32[]{:S(2)}) copy-start(f32[8192]{0:T(1024)} %get-tuple-element.162) | copy-start | bytes 98308
  (8 other events, 10.5 us)
Sparse Core Ops, SparseCore 0:
  9.6 67.6 all-gather.4
  79.5 135.0 all-gather.2
  360.3 86.8 reduce-scatter.7
  450.9 143.8 all-reduce.3
  597.0 50.3 reduce-scatter.5
  650.1 48.1 reduce-scatter.3
  705.8 120.5 all-reduce.5
